TPU v7x, 32 devices: a whole 2x2x4 slice. The times are simulated.
32 devices in a mesh: dp: 8 (over z, core), tensor: 4 (over y, x).
Axes of the slice: x: 2, y: 2, z: 4, core: 2. Of those that a mesh axis runs over, the one named last changes fastest.
Arguments:
- tokens: bfloat16 [8192, 2048], P('dp'), may hold values from -6 to 6
- cotangent: bfloat16 [8192, 2048], P('dp'), may hold values from -6 to 6
- seq_lengths: int32 [4], replicated, may hold values from 1536 to 2048, as said below
- slot_seq: int32 [4], replicated, may hold values from 0 to 3, each once
- w_query: float32 [2048, 2048], P('dp', 'tensor'), may hold values from -0.125 to 0.125
- w_key: float32 [2048, 2048], P('dp', 'tensor'), may hold values from -0.125 to 0.125
- w_value: float32 [2048, 2048], P('dp', 'tensor'), may hold values from -0.125 to 0.125
- b_query: float32 [2048], P('tensor'), may hold values from -3 to 3
- b_value: float32 [2048], P('tensor'), may hold values from -3 to 3
- w_out: float32 [2048, 2048], P('tensor', 'dp'), may hold values from -4 to 4
- b_out: float32 [2048], replicated, may hold values from -3 to 3
- ln1_gain: float32 [2048], replicated, may hold values from 0.5 to 1.5
- ln1_bias: float32 [2048], replicated, may hold values from -3 to 3
- w_inner: float32 [2048, 8192], P('dp', 'tensor'), may hold values from -0.125 to 0.125
- b_inner: float32 [8192], P('tensor'), may hold values from -3 to 3
- w_outer: float32 [8192, 2048], P('tensor', 'dp'), may hold values from -0.0625 to 0.0625
- b_outer: float32 [2048], replicated, may hold values from -3 to 3
- ln2_gain: float32 [2048], replicated, may hold values from 0.5 to 1.5
- ln2_bias: float32 [2048], replicated, may hold values from -3 to 3
Outputs:
- output: float32 [8192, 2048], P('dp')
- grad_tokens: float32 [8192, 2048], P('dp')
- grad_w_query: float32 [2048, 2048], P('dp', 'tensor')
- grad_w_key: float32 [2048, 2048], P('dp', 'tensor')
- grad_w_value: float32 [2048, 2048], P('dp', 'tensor')
- grad_b_query: float32 [2048], P('tensor')
- grad_b_value: float32 [2048], P('tensor')
- grad_w_out: float32 [2048, 2048], P('tensor', 'dp')
- grad_b_out: float32 [2048], replicated
- grad_ln1_gain: float32 [2048], replicated
- grad_ln1_bias: float32 [2048], replicated
- grad_w_inner: float32 [2048, 8192], P('dp', 'tensor')
- grad_b_inner: float32 [8192], P('tensor')
- grad_w_outer: float32 [8192, 2048], P('tensor', 'dp')
- grad_b_outer: float32 [2048], replicated
- grad_ln2_gain: float32 [2048], replicated
- grad_ln2_bias: float32 [2048], replicated
Inputs may be any that keep to these rules, and one draw needn't show every extreme that they name: `seq_lengths`: each sequence's valid tokens; some sequence has exactly 2048 and some exactly 1536. `slot_seq`: each sequence stands in exactly one slot.
All inputs are finite; a program needn't handle non-finite values.
Results may differ from a plain program's by a relative error of at most 0.019.
Values may be sent and summed in bfloat16 or wider, within the bound.
No kernel may reach another device: no remote copies, remote signals or barrier semaphores. Data moves between devices by JAX's collectives and lax.ppermute only.
A program may use at most 256 MiB of HBM per device.

v0:
```python
import jax
import jax.numpy as jnp
from jax import lax
from jax.sharding import PartitionSpec as P

HEAD_DIM = 128
SLOT = 2048
norm_eps = 1e-12


def passed_along(value, axis, steps):
    count = lax.axis_size(axis)
    leading, last = (max(0, -steps), min(count, count - steps))
    return lax.ppermute(value, axis, [(source, source + steps) for source in range(leading, last)])


def layer_norm(resid, gain, shift):
    center = resid - jnp.mean(resid, axis=-1, keepdims=True)
    spread = jnp.mean(center * center, axis=-1, keepdims=True)
    return center * lax.rsqrt(spread + norm_eps) * gain + shift


def gelu_tanh(inner):
    return 0.5 * inner * (1.0 + jnp.tanh(0.7978845608 * (inner + 0.044715 * inner * inner * inner)))


def mat_bf(left, right):
    return jnp.dot(left, right, preferred_element_type=jnp.float32)


def tensor_total(part):
    return lax.psum(part, "tensor")


def on_device(
    tokens,
    cotangent,
    seq_lengths,
    slot_seq,
    w_query,
    w_key,
    w_value,
    b_query,
    b_value,
    w_out,
    b_out,
    ln1_gain,
    ln1_bias,
    w_inner,
    b_inner,
    w_outer,
    b_outer,
    ln2_gain,
    ln2_bias,
):
    tok_rows = tokens.shape[0]
    shard_count = SLOT // tok_rows
    width_here = w_query.shape[1]
    heads_here = width_here // HEAD_DIM
    score_scale = HEAD_DIM ** (-0.5)
    block_rows = min(512, tok_rows)
    block_count = tok_rows // block_rows
    dp_place = lax.axis_index("dp")
    my_slot = dp_place // shard_count
    my_spot = dp_place % shard_count
    slot_ids = jnp.arange(slot_seq.shape[0])
    slot_lengths = jnp.sum(
        jnp.where(slot_seq[:, None] == slot_ids[None, :], seq_lengths[None, :], 0), axis=1
    )
    my_length = jnp.sum(jnp.where(slot_ids == my_slot, slot_lengths, 0))
    row_live = (my_spot * tok_rows + jnp.arange(tok_rows) < my_length).astype(jnp.float32)
    key_live = jnp.arange(SLOT) < my_length
    spot_ids = jnp.arange(shard_count)
    offset_list = [step_by for step_by in range(1 - shard_count, shard_count) if step_by != 0]
    own_hit = (spot_ids == my_spot)[:, None, None]
    tokens_wide = tokens.astype(jnp.float32)
    cot_wide = cotangent.astype(jnp.float32)
    full_query, full_key, full_value, full_out = (
        lax.all_gather(w_query.astype(jnp.bfloat16), "dp", axis=0, tiled=True),
        lax.all_gather(w_key.astype(jnp.bfloat16), "dp", axis=0, tiled=True),
        lax.all_gather(w_value.astype(jnp.bfloat16), "dp", axis=0, tiled=True),
        lax.all_gather(w_out.astype(jnp.bfloat16), "dp", axis=1, tiled=True),
    )
    query_rows = (mat_bf(tokens, full_query) + b_query).astype(jnp.bfloat16)
    key_rows = mat_bf(tokens, full_key).astype(jnp.bfloat16)
    value_rows = (mat_bf(tokens, full_value) + b_value).astype(jnp.bfloat16)
    empty_slab = jnp.zeros((shard_count, tok_rows, width_here), jnp.bfloat16)
    key_slab = jnp.where(own_hit, key_rows[None], empty_slab)
    value_slab = jnp.where(own_hit, value_rows[None], empty_slab)
    for step_by in offset_list:
        far_key, far_value = passed_along((key_rows, value_rows), "dp", step_by)
        far_hit = (spot_ids == my_spot - step_by)[:, None, None]
        key_slab = jnp.where(far_hit, far_key[None], key_slab)
        value_slab = jnp.where(far_hit, far_value[None], value_slab)
    slot_keys = key_slab.reshape(SLOT, heads_here, HEAD_DIM)
    slot_values = value_slab.reshape(SLOT, heads_here, HEAD_DIM)
    query_blocks = query_rows.reshape(block_count, block_rows, heads_here, HEAD_DIM)

    def score_block(query_part):
        scores = (
            jnp.einsum("qhd,khd->hqk", query_part, slot_keys, preferred_element_type=jnp.float32)
            * score_scale
        )
        return jnp.where(key_live[None, None, :], scores, -1e30)

    def forward_block(query_part):
        scores = score_block(query_part)
        top = jnp.max(scores, axis=-1, keepdims=True)
        expd = jnp.exp(scores - top)
        total = jnp.sum(expd, axis=-1, keepdims=True)
        probs = expd / total
        mixed = jnp.einsum(
            "hqk,khd->qhd",
            probs.astype(jnp.bfloat16),
            slot_values,
            preferred_element_type=jnp.float32,
        )
        return (mixed, top + jnp.log(total))

    mixed_blocks, lse_blocks = lax.map(forward_block, query_blocks)
    heads_rows = mixed_blocks.reshape(tok_rows, width_here).astype(jnp.bfloat16)
    attn_part = mat_bf(heads_rows, full_out)
    attn = tensor_total(attn_part) + b_out
    resid_one = tokens_wide + attn
    hidden, norm_one_back = jax.vjp(layer_norm, resid_one, ln1_gain, ln1_bias)
    hidden_low = hidden.astype(jnp.bfloat16)
    full_inner, full_outer = (
        lax.all_gather(w_inner.astype(jnp.bfloat16), "dp", axis=0, tiled=True),
        lax.all_gather(w_outer.astype(jnp.bfloat16), "dp", axis=1, tiled=True),
    )
    inner = mat_bf(hidden_low, full_inner) + b_inner
    act_low = gelu_tanh(inner).astype(jnp.bfloat16)
    outer_part = mat_bf(act_low, full_outer)
    outer = tensor_total(outer_part) + b_outer
    output, norm_two_back = jax.vjp(layer_norm, hidden + outer, ln2_gain, ln2_bias)
    grad_out = cot_wide * row_live[:, None]
    grad_two, grad_ln2_gain, grad_ln2_bias = norm_two_back(grad_out)
    back_inner, back_outer = (
        lax.all_gather(w_inner.astype(jnp.bfloat16), "dp", axis=0, tiled=True),
        lax.all_gather(w_outer.astype(jnp.bfloat16), "dp", axis=1, tiled=True),
    )
    outer_low = grad_two.astype(jnp.bfloat16)
    grad_b_outer = jnp.sum(grad_two, axis=0)
    grad_w_outer = jnp.einsum("tf,td->fd", act_low, outer_low, preferred_element_type=jnp.float32)
    grad_act = jnp.einsum("td,fd->tf", outer_low, back_outer, preferred_element_type=jnp.float32)
    gelu_value, gelu_back = jax.vjp(gelu_tanh, inner)
    inner_low = gelu_back(grad_act)[0].astype(jnp.bfloat16)
    grad_b_inner = jnp.sum(inner_low.astype(jnp.float32), axis=0)
    grad_w_inner = jnp.einsum(
        "td,tf->df", hidden_low, inner_low, preferred_element_type=jnp.float32
    )
    grad_w_inner, grad_w_outer = (
        lax.psum_scatter(
            grad_w_inner.astype(jnp.bfloat16), "dp", scatter_dimension=0, tiled=True
        ).astype(jnp.float32),
        lax.psum_scatter(
            grad_w_outer.astype(jnp.bfloat16), "dp", scatter_dimension=1, tiled=True
        ).astype(jnp.float32),
    )
    hidden_part = jnp.einsum("tf,df->td", inner_low, back_inner, preferred_element_type=jnp.float32)
    grad_hidden = grad_two + tensor_total(hidden_part)
    grad_one, grad_ln1_gain, grad_ln1_bias = norm_one_back(grad_hidden)
    attn_low = grad_one.astype(jnp.bfloat16)
    grad_b_out = jnp.sum(grad_one, axis=0)
    back_query, back_key, back_value, back_out = (
        lax.all_gather(w_query.astype(jnp.bfloat16), "dp", axis=0, tiled=True),
        lax.all_gather(w_key.astype(jnp.bfloat16), "dp", axis=0, tiled=True),
        lax.all_gather(w_value.astype(jnp.bfloat16), "dp", axis=0, tiled=True),
        lax.all_gather(w_out.astype(jnp.bfloat16), "dp", axis=1, tiled=True),
    )
    grad_w_out = jnp.einsum("tc,td->cd", heads_rows, attn_low, preferred_element_type=jnp.float32)
    mixed_low = jnp.einsum(
        "td,cd->tc", attn_low, back_out, preferred_element_type=jnp.float32
    ).astype(jnp.bfloat16)
    grad_blocks = mixed_low.reshape(block_count, block_rows, heads_here, HEAD_DIM)

    def backward_block(carry, inputs):
        key_sum, value_sum = carry
        query_part, grad_part, lse_part = inputs
        probs = jnp.exp(score_block(query_part) - lse_part)
        grad_probs = jnp.einsum(
            "qhd,khd->hqk", grad_part, slot_values, preferred_element_type=jnp.float32
        )
        inner_sum = jnp.sum(probs * grad_probs, axis=-1, keepdims=True)
        score_low = (probs * (grad_probs - inner_sum)).astype(jnp.bfloat16)
        grad_query = (
            jnp.einsum("hqk,khd->qhd", score_low, slot_keys, preferred_element_type=jnp.float32)
            * score_scale
        )
        key_sum = (
            key_sum
            + jnp.einsum("hqk,qhd->khd", score_low, query_part, preferred_element_type=jnp.float32)
            * score_scale
        )
        value_sum = value_sum + jnp.einsum(
            "hqk,qhd->khd",
            probs.astype(jnp.bfloat16),
            grad_part,
            preferred_element_type=jnp.float32,
        )
        return ((key_sum, value_sum), grad_query)

    zero_slab = jnp.zeros((SLOT, heads_here, HEAD_DIM), jnp.float32)
    (key_sum, value_sum), grad_query_blocks = lax.scan(
        backward_block, (zero_slab, zero_slab), (query_blocks, grad_blocks, lse_blocks)
    )
    key_grad_slab = key_sum.reshape(shard_count, tok_rows, width_here)
    value_grad_slab = value_sum.reshape(shard_count, tok_rows, width_here)
    grad_key = jnp.sum(jnp.where(own_hit, key_grad_slab, 0.0), axis=0)
    grad_value = jnp.sum(jnp.where(own_hit, value_grad_slab, 0.0), axis=0)
    for step_by in offset_list:
        far_hit = (spot_ids == my_spot - step_by)[:, None, None]
        send_key = jnp.sum(jnp.where(far_hit, key_grad_slab, 0.0), axis=0)
        send_value = jnp.sum(jnp.where(far_hit, value_grad_slab, 0.0), axis=0)
        back_key_rows, back_value_rows = (
            passed_along(send_key.astype(jnp.bfloat16), "dp", -step_by).astype(send_key.dtype),
            passed_along(send_value.astype(jnp.bfloat16), "dp", -step_by).astype(send_value.dtype),
        )
        grad_key = grad_key + back_key_rows
        grad_value = grad_value + back_value_rows
    query_low = grad_query_blocks.reshape(tok_rows, width_here).astype(jnp.bfloat16)
    key_low = grad_key.astype(jnp.bfloat16)
    value_low = grad_value.astype(jnp.bfloat16)
    grad_w_query = jnp.einsum("td,tc->dc", tokens, query_low, preferred_element_type=jnp.float32)
    grad_w_key = jnp.einsum("td,tc->dc", tokens, key_low, preferred_element_type=jnp.float32)
    grad_w_value = jnp.einsum("td,tc->dc", tokens, value_low, preferred_element_type=jnp.float32)
    grad_b_query = jnp.sum(query_low.astype(jnp.float32), axis=0)
    grad_b_value = jnp.sum(value_low.astype(jnp.float32), axis=0)
    input_part = jnp.einsum("tc,dc->td", query_low, back_query, preferred_element_type=jnp.float32)
    input_part = input_part + jnp.einsum(
        "tc,dc->td", key_low, back_key, preferred_element_type=jnp.float32
    )
    input_part = input_part + jnp.einsum(
        "tc,dc->td", value_low, back_value, preferred_element_type=jnp.float32
    )
    grad_tokens = grad_one + tensor_total(input_part)
    grad_w_query, grad_w_key, grad_w_value, grad_w_out = (
        lax.psum_scatter(
            grad_w_query.astype(jnp.bfloat16), "dp", scatter_dimension=0, tiled=True
        ).astype(jnp.float32),
        lax.psum_scatter(
            grad_w_key.astype(jnp.bfloat16), "dp", scatter_dimension=0, tiled=True
        ).astype(jnp.float32),
        lax.psum_scatter(
            grad_w_value.astype(jnp.bfloat16), "dp", scatter_dimension=0, tiled=True
        ).astype(jnp.float32),
        lax.psum_scatter(
            grad_w_out.astype(jnp.bfloat16), "dp", scatter_dimension=1, tiled=True
        ).astype(jnp.float32),
    )
    (
        grad_b_query,
        grad_b_value,
        grad_b_inner,
        grad_b_out,
        grad_b_outer,
        grad_ln1_gain,
        grad_ln1_bias,
        grad_ln2_gain,
        grad_ln2_bias,
    ) = (
        lax.psum(grad_b_query.astype(jnp.bfloat16), "dp").astype(jnp.float32),
        lax.psum(grad_b_value.astype(jnp.bfloat16), "dp").astype(jnp.float32),
        lax.psum(grad_b_inner.astype(jnp.bfloat16), "dp").astype(jnp.float32),
        lax.psum(grad_b_out.astype(jnp.bfloat16), "dp").astype(jnp.float32),
        lax.psum(grad_b_outer.astype(jnp.bfloat16), "dp").astype(jnp.float32),
        lax.psum(grad_ln1_gain.astype(jnp.bfloat16), "dp").astype(jnp.float32),
        lax.psum(grad_ln1_bias.astype(jnp.bfloat16), "dp").astype(jnp.float32),
        lax.psum(grad_ln2_gain.astype(jnp.bfloat16), "dp").astype(jnp.float32),
        lax.psum(grad_ln2_bias.astype(jnp.bfloat16), "dp").astype(jnp.float32),
    )
    return (
        output,
        grad_tokens,
        grad_w_query,
        grad_w_key,
        grad_w_value,
        grad_b_query,
        grad_b_value,
        grad_w_out,
        grad_b_out,
        grad_ln1_gain,
        grad_ln1_bias,
        grad_w_inner,
        grad_b_inner,
        grad_w_outer,
        grad_b_outer,
        grad_ln2_gain,
        grad_ln2_bias,
    )


def solution(mesh):
    return jax.shard_map(
        on_device,
        mesh=mesh,
        in_specs=(
            P("dp", None),
            P("dp", None),
            P(),
            P(),
            P("dp", "tensor"),
            P("dp", "tensor"),
            P("dp", "tensor"),
            P("tensor"),
            P("tensor"),
            P("tensor", "dp"),
            P(),
            P(),
            P(),
            P("dp", "tensor"),
            P("tensor"),
            P("tensor", "dp"),
            P(),
            P(),
            P(),
        ),
        out_specs=(
            P("dp", None),
            P("dp", None),
            P("dp", "tensor"),
            P("dp", "tensor"),
            P("dp", "tensor"),
            P("tensor"),
            P("tensor"),
            P("tensor", "dp"),
            P(),
            P(),
            P(),
            P("dp", "tensor"),
            P("tensor"),
            P("tensor", "dp"),
            P(),
            P(),
            P(),
        ),
        check_vma=False,
    )
```

profile of v0, /device:TPU:0, one launch (start us, length us, event | category | flops | bytes accessed | tf_op | source)
XLA Modules:
  0.0 1807.7 jit_solution(10736105335624038911)
XLA Ops:
  14.7 27.4 %all-gather.9.cloned.1.call-done = bf16[2048,512]{1,0:T(8,128)(2,1)} async-done(((bf16[256,512]{1,0:T(8,128)(2,1)}), bf16[2048,512]{1,0:T(8,128)(2,1)}) %all-gather.9.cloned.1.call-update) | async-done | bytes 2097168 | tf_op jit(solution)/shard_map/all_gather | solution.py:80
  52.8 25.2 %all-gather.11.cloned.1.call-done = bf16[2048,512]{1,0:T(8,128)(2,1)} async-done(((bf16[256,512]{1,0:T(8,128)(2,1)}), bf16[2048,512]{1,0:T(8,128)(2,1)}) %all-gather.11.cloned.1.call-update) | async-done | bytes 2097168 | tf_op jit(solution)/shard_map/all_gather | solution.py:81
  90.7 26.6 %all-gather.7.cloned.1.call-done = bf16[2048,512]{1,0:T(8,128)(2,1)} async-done(((bf16[256,512]{1,0:T(8,128)(2,1)}), bf16[2048,512]{1,0:T(8,128)(2,1)}) %all-gather.7.cloned.1.call-update) | async-done | bytes 2097168 | tf_op jit(solution)/shard_map/all_gather | solution.py:79
  127.6 128.1 %while.31 = (s32[]{:T(128)}, bf16[2,512,4,128]{3,1,2,0:T(8,128)(2,1)}, f32[2,4,512,1]{2,1,3,0:T(4,128)S(1)}, bf16[2,512,4,128]{3,1,2,0:T(8,128)(2,1)}, s32[]{:T(...) while((s32[]{:T(128)}, ...), condition=%wide.region_5.6_spmd.clone.clone, body=%wide.region_2.5_spmd.clone.clone.sunk | while | flops 2204106752 | bytes 137967920 | solution.py:120
  164.7 14.5 select_select_fusion.6
  228.7 14.5 select_select_fusion.6
  271.7 169.3 %all-reduce.6.cloned.1.call-done = f32[1024,2048]{1,0:T(8,128)} async-done(((f32[1024,2048]{1,0:T(8,128)}), f32[1024,2048]{1,0:T(8,128)}) %all-reduce.6.cloned.1.call-update) | async-done | bytes 8388624 | tf_op jit(solution)/shard_map/psum | solution.py:32
  451.1 74.8 %all-gather.15.cloned.1.call-done = bf16[2048,2048]{1,0:T(8,128)(2,1)} async-done(((bf16[256,2048]{1,0:T(8,128)(2,1)}), bf16[2048,2048]{1,0:T(8,128)(2,1)}) %all-gather.15.cloned.1.call-update) | async-done | bytes 8388624 | tf_op jit(solution)/shard_map/all_gather | solution.py:128
  525.9 15.8 fusion.87
  541.7 67.5 %all-gather.17.cloned.1.call-done = bf16[2048,2048]{1,0:T(8,128)(2,1)} async-done(((bf16[2048,256]{1,0:T(8,128)(2,1)}), bf16[2048,2048]{1,0:T(8,128)(2,1)}) %all-gather.17.cloned.1.call-update) | async-done | bytes 8388624 | tf_op jit(solution)/shard_map/all_gather | solution.py:129
  609.2 17.3 fusion.85
  627.5 169.5 %all-reduce.8.cloned.1.call-done = f32[1024,2048]{1,0:T(8,128)} async-done(((f32[1024,2048]{1,0:T(8,128)}), f32[1024,2048]{1,0:T(8,128)}) %all-reduce.8.cloned.1.call-update) | async-done | bytes 8388624 | tf_op jit(solution)/shard_map/psum | solution.py:32
  818.5 23.4 %fusion.94 = (bf16[2048]{0:T(1024)(128)(2,1)}, bf16[1024,2048]{1,0:T(8,128)(2,1)}) fusion(bf16[2048,2048]{1,0:T(8,128)(2,1)} %all-gather.17.cloned.1.call-done, f32[1024,2048]{1,0:T(8,128)} %get-tuple-element.655, f32[1024]{0:T(1024)S(1)} %negate_multiply_fusion.1, f32[1024,2048]{1,0:T(8,128)} %fusion.87, f32[2048]{0:T(1024)S(1)} %copy-done.68), kind=kOutput, calls=%fused_computation.149 | convolution fusion | flops 8648652800 | bytes 29376512 | tf_op jit(solution)/shard_map/td,fd->tf/dot_general | solution.py:145
  842.0 14.5 fusion.95
  856.5 172.9 %all-reduce.10.cloned.1.call-done = f32[1024,2048]{1,0:T(8,128)} async-done(((f32[1024,2048]{1,0:T(8,128)}), f32[1024,2048]{1,0:T(8,128)}) %all-reduce.10.cloned.1.call-update) | async-done | bytes 8388624 | tf_op jit(solution)/shard_map/psum | solution.py:32
  1029.4 11.8 multiply_reduce_fusion.2
  1061.4 165.6 %while.32 = (s32[]{:T(128)}, f32[2048,4,128]{0,2,1:T(8,128)}, f32[2048,4,128]{0,2,1:T(8,128)}, bf16[2,512,4,128]{3,1,2,0:T(8,128)(2,1)}, bf16[2,512,4,128]{3,1,2...) while((s32[]{:T(128)}, f32[2048,4,128]{0,2,1:T(8,128)}, ...), condition=%wide.region_19.20_spmd.clone.clone.clone, body=%wide.region_17.19_spmd.clone.clone.clone.sunk | while | flops 5443420160 | bytes 367073888 | solution.py:204
  1082.1 14.4 select_select_fusion.7
  1111.6 11.6 multiply_reduce_fusion.8
  1123.2 12.9 multiply_convert_fusion.5
  1163.9 14.4 select_select_fusion.7
  1194.9 11.6 multiply_reduce_fusion.8
  1206.5 12.9 multiply_convert_fusion.5
  1249.2 47.1 %select_reduce_fusion.4 = (bf16[1024,512]{0,1:T(8,128)(2,1)}, bf16[1024,512]{0,1:T(8,128)(2,1)}, f32[1024,512]{0,1:T(8,128)S(1)}, f32[1024,512]{0,1:T(8,128)S(1)...) fusion(f32[2,1024,512]{1,0,2:T(2,128)} %reshape.188, pred[2]{0:T(512)(128)(4,1)S(1)} %copy-done.63, ...), kind=kLoop, calls=%fused_computation.97 | loop fusion | flops 9437184 | bytes 16777222 | tf_op jit(solution)/shard_map/reduce_sum | solution.py:213
  1307.3 12.6 collective-permute-start.4
  1334.2 15.4 convolution_convert_fusion.1
  1350.3 20.0 %convolution_convert_fusion = bf16[2048,2048]{1,0:T(8,128)(2,1)} fusion(f32[1024,2048]{1,0:T(8,128)} %get-tuple-element.655, f32[1024]{0:T(1024)S(1)} %copy-done.54, f32[1024,2048]{1,0:T(8,128)} %fusion.87, f32[2048]{0:T(1024)S(1)} %copy-done.69), kind=kOutput, calls=%fused_computation.84 | convolution fusion | flops 8619294720 | bytes 25178112 | tf_op jit(solution)/shard_map/tf,td->fd/dot_general | solution.py:144
  1391.1 10.2 reduce-scatter.9.cloned.1.call-done
  1403.1 88.7 %reduce-scatter.15.cloned.1.call-done = bf16[256,2048]{1,0:T(8,128)(2,1)} async-done(((bf16[2048,2048]{1,0:T(8,128)(2,1)}), bf16[256,2048]{1,0:T(8,128)(2,1)}) %reduce-scatter.15.cloned.1.call-update) | async-done | bytes 1048592 | tf_op jit(solution)/shard_map/reduce_scatter | solution.py:153
  1494.7 87.5 %reduce-scatter.17.cloned.1.call-done = bf16[2048,256]{1,0:T(8,128)(2,1)} async-done(((bf16[2048,2048]{1,0:T(8,128)(2,1)}), bf16[2048,256]{1,0:T(8,128)(2,1)}) %reduce-scatter.17.cloned.1.call-update) | async-done | bytes 1048592 | tf_op jit(solution)/shard_map/reduce_scatter | solution.py:156
  1584.9 172.1 %all-reduce.12.cloned.1.call-done = f32[1024,2048]{1,0:T(8,128)} async-done(((f32[1024,2048]{1,0:T(8,128)}), f32[1024,2048]{1,0:T(8,128)}) %all-reduce.12.cloned.1.call-update) | async-done | bytes 8388624 | tf_op jit(solution)/shard_map/psum | solution.py:32
  1767.0 28.6 %all-reduce = (bf16[512]{0:T(512)(128)(2,1)S(1)}, bf16[512]{0:T(512)(128)(2,1)S(1)}, bf16[2048]{0:T(1024)(128)(2,1)S(1)}, bf16[2048]{0:T(1024)(128)(2,1)S(1)}, b...) all-reduce(bf16[512]{0:T(512)(128)(2,1)S(1)} %bitcast.117, ...), channel_id=1, replica_groups=mesh['dp'=8,'tensor'=4] {'dp'}, use_global_device_ids=true, to_apply=%region_31.32 | all-reduce | flops 15360 | bytes 61440 | tf_op jit(solution)/shard_map/psum | solution.py:262
  (384 shorter events, 386.8 us)
Async XLA Ops:
  7.2 34.8 %all-gather.9.cloned.1.call-start = ((), (), s32[]{:S(2)}) async-start(), calls=%async_computation.7 | async-start | bytes 2359296 | tf_op jit(solution)/shard_map/all_gather | solution.py:80
  9.0 68.9 %all-gather.11.cloned.1.call-start = ((), (), s32[]{:S(2)}) async-start(), calls=%async_computation.8 | async-start | bytes 2359296 | tf_op jit(solution)/shard_map/all_gather | solution.py:81
  10.9 106.4 %all-gather.7.cloned.1.call-start = ((), (), s32[]{:S(2)}) async-start(), calls=%async_computation.6 | async-start | bytes 2359296 | tf_op jit(solution)/shard_map/all_gather | solution.py:79
  12.7 245.8 %all-gather.13.cloned.1.call-start = ((), (), s32[]{:S(2)}) async-start(), calls=%async_computation.9 | async-start | bytes 2359296 | tf_op jit(solution)/shard_map/all_gather | solution.py:82
  14.6 426.4 %all-reduce.6.cloned.1.call-start = ((), (), s32[]{:S(2)}) async-start(), calls=%async_computation.10 | async-start | bytes 16777216 | tf_op jit(solution)/shard_map/psum | solution.py:32
  47.3 79.2 %collective-permute-start.1 = (bf16[1024,512]{1,0:T(8,128)(2,1)S(1)}, bf16[1024,512]{1,0:T(8,128)(2,1)}, u32[]{:S(2)}, u32[]{:S(2)}) collective-permute-start(bf16[1024,512]{1,0:T(8,128)(2,1)S(1)} %convolution_convert_fusion.7), channel_id=1, source_target_pairs={{4,0},{8,4},{12,8},{16,12},{20,16},{24,20},{28,24},{5,1},{9,5},{13... | collective-permute-start | bytes 3145736 | tf_op jit(solution)/shard_map/ppermute | solution.py:14
  48.7 77.7 %collective-permute-start = (bf16[1024,512]{1,0:T(8,128)(2,1)S(1)}, bf16[1024,512]{1,0:T(8,128)(2,1)}, u32[]{:S(2)}, u32[]{:S(2)}) collective-permute-start(bf16[1024,512]{1,0:T(8,128)(2,1)S(1)} %convolution_convert_fusion.7), channel_id=1, source_target_pairs={{0,4},{4,8},{8,12},{12,16},{16,20},{20,24},{24,28},{1,5},{5,9},{9,... | collective-permute-start | bytes 3145736 | tf_op jit(solution)/shard_map/ppermute | solution.py:14
  83.2 43.3 %collective-permute-start.3 = (bf16[1024,512]{1,0:T(8,128)(2,1)S(1)}, bf16[1024,512]{1,0:T(8,128)(2,1)}, u32[]{:S(2)}, u32[]{:S(2)}) collective-permute-start(bf16[1024,512]{1,0:T(8,128)(2,1)S(1)} %add_convert_fusion.4), channel_id=1, source_target_pairs={{4,0},{8,4},{12,8},{16,12},{20,16},{24,20},{28,24},{5,1},{9,5},{13... | collective-permute-start | bytes 3145736 | tf_op jit(solution)/shard_map/ppermute | solution.py:14
  84.5 42.0 %collective-permute-start.2 = (bf16[1024,512]{1,0:T(8,128)(2,1)S(1)}, bf16[1024,512]{1,0:T(8,128)(2,1)}, u32[]{:S(2)}, u32[]{:S(2)}) collective-permute-start(bf16[1024,512]{1,0:T(8,128)(2,1)S(1)} %add_convert_fusion.4), channel_id=1, source_target_pairs={{0,4},{4,8},{8,12},{12,16},{16,20},{20,24},{24,28},{1,5},{5,9},{9,... | collective-permute-start | bytes 3145736 | tf_op jit(solution)/shard_map/ppermute | solution.py:14
  255.7 191.0 %copy-start.12 = (bf16[1024,512]{1,0:T(8,128)(2,1)}, bf16[1024,512]{1,0:T(8,128)(2,1)S(1)}, u32[]{:S(2)}) copy-start(bf16[1024,512]{1,0:T(8,128)(2,1)S(1)} %get-tuple-element.1027) | copy-start | bytes 3145732
  265.9 260.0 %all-gather.15.cloned.1.call-start = ((), (), s32[]{:S(2)}) async-start(), calls=%async_computation.11 | async-start | bytes 9437184 | tf_op jit(solution)/shard_map/all_gather | solution.py:128
  268.7 340.5 %all-gather.17.cloned.1.call-start = ((), (), s32[]{:S(2)}) async-start(), calls=%async_computation.12 | async-start | bytes 9437184 | tf_op jit(solution)/shard_map/all_gather | solution.py:129
  271.5 525.5 %all-reduce.8.cloned.1.call-start = ((), (), s32[]{:S(2)}) async-start(), calls=%async_computation.13 | async-start | bytes 16777216 | tf_op jit(solution)/shard_map/psum | solution.py:32
  446.8 594.4 %copy-start.39 = (f32[1024]{0:T(1024)}, f32[1024]{0:T(1024)S(1)}, u32[]{:S(2)}) copy-start(f32[1024]{0:T(1024)S(1)} %broadcast_multiply_fusion.1) | copy-start | bytes 12292
  451.1 590.1 %copy-start.43 = (f32[1024]{0:T(1024)}, f32[1024]{0:T(1024)S(1)}, u32[]{:S(2)}) copy-start(f32[1024]{0:T(1024)S(1)} %fusion.81) | copy-start | bytes 12292
  626.6 402.8 %all-reduce.10.cloned.1.call-start = ((), (), s32[]{:S(2)}) async-start(), calls=%async_computation.14 | async-start | bytes 16777216 | tf_op jit(solution)/shard_map/psum | solution.py:32
  818.5 210.9 %copy-start.53 = (f32[1024]{0:T(1024)}, f32[1024]{0:T(1024)S(1)}, u32[]{:S(2)}) copy-start(f32[1024]{0:T(1024)S(1)} %negate_multiply_fusion.1) | copy-start | bytes 12292
  856.5 529.0 %reduce-scatter.13.cloned.1.call-start = ((), (), s32[]{:S(2)}) async-start(), calls=%async_computation.19 | async-start | bytes 2359296 | tf_op jit(solution)/shard_map/reduce_scatter | solution.py:247
  1060.2 327.1 %reduce-scatter.7.cloned.1.call-start = ((), (), s32[]{:S(2)}) async-start(), calls=%async_computation.16 | async-start | bytes 2359296 | tf_op jit(solution)/shard_map/reduce_scatter | solution.py:238
  1236.0 153.2 %reduce-scatter.11.cloned.1.call-start = ((), (), s32[]{:S(2)}) async-start(), calls=%async_computation.18 | async-start | bytes 2359296 | tf_op jit(solution)/shard_map/reduce_scatter | solution.py:244
  1296.3 4.6 collective-permute-start.7
  1297.6 5.5 collective-permute-start.6
  1307.3 94.0 %reduce-scatter.9.cloned.1.call-start = ((), (), s32[]{:S(2)}) async-start(), calls=%async_computation.17 | async-start | bytes 2359296 | tf_op jit(solution)/shard_map/reduce_scatter | solution.py:241
  1307.3 15.0 collective-permute-start.4
  1319.9 6.7 collective-permute-start.5
  1334.1 157.8 %reduce-scatter.15.cloned.1.call-start = ((), (), s32[]{:S(2)}) async-start(), calls=%async_computation.20 | async-start | bytes 9437184 | tf_op jit(solution)/shard_map/reduce_scatter | solution.py:153
  1349.6 232.5 %reduce-scatter.17.cloned.1.call-start = ((), (), s32[]{:S(2)}) async-start(), calls=%async_computation.21 | async-start | bytes 9437184 | tf_op jit(solution)/shard_map/reduce_scatter | solution.py:156
  1370.3 386.7 %all-reduce.12.cloned.1.call-start = ((), (), s32[]{:S(2)}) async-start(), calls=%async_computation.15 | async-start | bytes 16777216 | tf_op jit(solution)/shard_map/psum | solution.py:32
  1384.1 372.9 %copy-start.46 = (f32[1024]{0:T(1024)S(1)}, f32[1024]{0:T(1024)}, u32[]{:S(2)}) copy-start(f32[1024]{0:T(1024)} %copy-done.45) | copy-start | bytes 12292
  1584.8 182.2 %copy-start.51 = (bf16[2048]{0:T(1024)(128)(2,1)S(1)}, bf16[2048]{0:T(1024)(128)(2,1)}, u32[]{:S(2)}) copy-start(bf16[2048]{0:T(1024)(128)(2,1)} %get-tuple-element.567) | copy-start | bytes 12292
  1584.8 182.2 %copy-start.52 = (bf16[2048]{0:T(1024)(128)(2,1)S(1)}, bf16[2048]{0:T(1024)(128)(2,1)}, u32[]{:S(2)}) copy-start(bf16[2048]{0:T(1024)(128)(2,1)} %get-tuple-element.669) | copy-start | bytes 12292
  1584.9 182.2 %copy-start.64 = (bf16[2048]{0:T(1024)(128)(2,1)S(1)}, bf16[2048]{0:T(1024)(128)(2,1)}, u32[]{:S(2)}) copy-start(bf16[2048]{0:T(1024)(128)(2,1)} %get-tuple-element.672) | copy-start | bytes 12292
  (85 other events, 1895.4 us)
Sparse Core Ops, SparseCore 0:
  10.2 31.7 all-gather.8
  44.2 33.7 all-gather.10
  80.1 37.1 all-gather.6
  119.3 33.6 all-gather.12
  266.0 174.9 all-reduce.5
  443.1 82.7 all-gather.14
  528.1 81.0 all-gather.16
  626.7 170.2 all-reduce.7
  856.6 172.7 all-reduce.9
  1060.3 36.5 reduce-scatter.12
  1236.1 36.5 reduce-scatter.6
  1307.4 52.8 reduce-scatter.10
  1363.2 37.9 reduce-scatter.8
  1403.5 88.3 reduce-scatter.14
  1494.1 87.9 reduce-scatter.16
  1586.5 170.4 all-reduce.11
where the time goes:
time: 1810 us
  waiting for transfers between devices  1100 us (61%)
  matrix products  235 us (13%)
  other arithmetic  222 us (12%)
  local copies, waits for them, and re-layouts  176 us (10%)
  starting transfers between devices  30.5 us (2%)
  blocking collectives  28.6 us (2%)
    psum x4, waiting for transfers between devices, tensor_total(): return lax.psum(part, 'tensor')  684 us
    reduce_scatter x1, waiting for transfers between devices, on_device(): lax.psum_scatter(grad_w_inner.astype(jnp.bfloat16), 'dp', scatter_dimensi...  88.7 us
    reduce_scatter x1, waiting for transfers between devices, on_device(): lax.psum_scatter(grad_w_outer.astype(jnp.bfloat16), 'dp', scatter_dimensi...  87.5 us
    all_gather x1, waiting for transfers between devices, on_device(): lax.all_gather(w_inner.astype(jnp.bfloat16), 'dp', axis=0, tiled=True)  74.8 us
    all_gather x1, waiting for transfers between devices, on_device(): lax.all_gather(w_outer.astype(jnp.bfloat16), 'dp', axis=1, tiled=True)  67.5 us
    select_n x4, other arithmetic, on_device(): key_slab = jnp.where(far_hit, far_key[None], key_slab)  57.8 us
    dot_general x6, matrix products, mat_bf(): return jnp.dot(left, right, preferred_element_type=jnp.float32)  57 us
    reduce_sum x1, other arithmetic, on_device(): send_key = jnp.sum(jnp.where(far_hit, key_grad_slab, 0.0), axis=0)  47.1 us
  transfers between devices with their start and end apart: 24, of which 15 were waited for; matrix products, arithmetic and copies ran while one was open for 26% of the time, Pallas kernels for 0%

commit v1 on v0

--- a/solution.py
+++ b/solution.py
@@ -29,7 +29,7 @@
 
 
 def tensor_total(part):
-    return lax.psum(part, "tensor")
+    return jnp.sum(lax.all_gather(part, "tensor"), axis=0)
 
 
 def on_device(

time: 1810 us -> 2240 us (1.24)
  waiting for transfers between devices: 1100 us -> 1400 us
  other arithmetic: 222 us -> 288 us
  matrix products: 235 us -> 271 us
  local copies, waits for them, and re-layouts: 176 us -> 200 us
    all_gather x0 -> x4, waiting for transfers between devices: none -> 1150 us  [tensor_total(): return jnp.sum(lax.all_gather(part, 'tensor'), axis=0)]
    psum x4 -> x0, waiting for transfers between devices: 684 us -> none  [tensor_total(): return lax.psum(part, 'tensor')]
    reduce_scatter x1, waiting for transfers between devices: 88.7 us -> 0.01 us  [on_device(): lax.psum_scatter(grad_w_inner.astype(jnp.bfloat16), 'dp', scatter_dimensi...]
    reduce_scatter x1, waiting for transfers between devices: 87.5 us -> 0.02 us  [on_device(): lax.psum_scatter(grad_w_outer.astype(jnp.bfloat16), 'dp', scatter_dimensi...]
    reduce_sum x0 -> x4, other arithmetic: none -> 66.4 us  [tensor_total(): return jnp.sum(lax.all_gather(part, 'tensor'), axis=0)]
    reduce_scatter x1, waiting for transfers between devices: 10.2 us -> 38.7 us  [on_device(): lax.psum_scatter(grad_w_key.astype(jnp.bfloat16), 'dp', scatter_dimension...]
  transfers between devices with their start and end apart: 24 -> 24, of which waited for: 15 -> 15; matrix products, arithmetic and copies ran while one was open for 26% -> 27% of each run, Pallas kernels for 0% -> 0%
where the time goes in v1:
time: 2240 us; the launch traced here: 2230 us
  waiting for transfers between devices  1400 us (62%)
  other arithmetic  288 us (13%)
  matrix products  271 us (12%)
  local copies, waits for them, and re-layouts  200 us (9%)
  blocking collectives  28.6 us (1%)
  starting transfers between devices  27.3 us (1%)
    all_gather x4, waiting for transfers between devices, tensor_total(): return jnp.sum(lax.all_gather(part, 'tensor'), axis=0)  1150 us
    all_gather x1, waiting for transfers between devices, on_device(): lax.all_gather(w_outer.astype(jnp.bfloat16), 'dp', axis=1, tiled=True)  67.4 us
    reduce_sum x4, other arithmetic, tensor_total(): return jnp.sum(lax.all_gather(part, 'tensor'), axis=0)  66.4 us
    select_n x4, other arithmetic, on_device(): key_slab = jnp.where(far_hit, far_key[None], key_slab)  57.7 us
    dot_general x6, matrix products, mat_bf(): return jnp.dot(left, right, preferred_element_type=jnp.float32)  57.3 us
    all_gather x1, waiting for transfers between devices, on_device(): lax.all_gather(w_inner.astype(jnp.bfloat16), 'dp', axis=0, tiled=True)  56.1 us
    broadcast_in_dim x16, local copies, waits for them, and re-layouts, on_device(): value_slab = jnp.where(far_hit, far_value[None], value_slab)  53.3 us
    reduce_sum x1, other arithmetic, on_device(): send_key = jnp.sum(jnp.where(far_hit, key_grad_slab, 0.0), axis=0)  47 us
  transfers between devices with their start and end apart: 24, of which 15 were waited for; matrix products, arithmetic and copies ran while one was open for 27% of the time, Pallas kernels for 0%

profile of v1, /device:TPU:0, one launch (start us, length us, event | category | flops | bytes accessed | tf_op | source)
XLA Modules:
  0.0 2230.5 jit_solution(3793240282463763023)
XLA Ops:
  14.7 27.4 %all-gather.17.cloned.1.call-done = bf16[2048,512]{1,0:T(8,128)(2,1)} async-done(((bf16[256,512]{1,0:T(8,128)(2,1)}), bf16[2048,512]{1,0:T(8,128)(2,1)}) %all-gather.17.cloned.1.call-update) | async-done | bytes 2097168 | tf_op jit(solution)/shard_map/all_gather | solution.py:80
  50.9 26.9 %all-gather.19.cloned.1.call-done = bf16[2048,512]{1,0:T(8,128)(2,1)} async-done(((bf16[256,512]{1,0:T(8,128)(2,1)}), bf16[2048,512]{1,0:T(8,128)(2,1)}) %all-gather.19.cloned.1.call-update) | async-done | bytes 2097168 | tf_op jit(solution)/shard_map/all_gather | solution.py:81
  89.8 27.3 %all-gather.15.cloned.1.call-done = bf16[2048,512]{1,0:T(8,128)(2,1)} async-done(((bf16[256,512]{1,0:T(8,128)(2,1)}), bf16[2048,512]{1,0:T(8,128)(2,1)}) %all-gather.15.cloned.1.call-update) | async-done | bytes 2097168 | tf_op jit(solution)/shard_map/all_gather | solution.py:79
  129.3 128.8 %while.31 = (s32[]{:T(128)}, bf16[2,512,4,128]{3,1,2,0:T(8,128)(2,1)}, f32[2,4,512,1]{2,1,3,0:T(4,128)S(1)}, bf16[2,512,4,128]{3,1,2,0:T(8,128)(2,1)}, s32[]{:T(...) while((s32[]{:T(128)}, ...), condition=%wide.region_5.6_spmd.clone.clone, body=%wide.region_2.5_spmd.clone.clone.sunk | while | flops 2204106752 | bytes 137968432 | solution.py:120
  166.7 14.4 select_select_fusion.6
  231.1 14.4 select_select_fusion.6
  275.4 294.7 %all-gather.27.cloned.1.call-done = f32[4096,2048]{1,0:T(8,128)} async-done(((f32[1024,2048]{1,0:T(8,128)}), f32[4096,2048]{1,0:T(8,128)}) %all-gather.27.cloned.1.call-update) | async-done | bytes 33554448 | tf_op jit(solution)/shard_map/all_gather | solution.py:32
  570.0 17.3 reduce_sum.324
  598.1 56.1 %all-gather.23.cloned.1.call-done = bf16[2048,2048]{1,0:T(8,128)(2,1)} async-done(((bf16[256,2048]{1,0:T(8,128)(2,1)}), bf16[2048,2048]{1,0:T(8,128)(2,1)}) %all-gather.23.cloned.1.call-update) | async-done | bytes 8388624 | tf_op jit(solution)/shard_map/all_gather | solution.py:128
  654.2 15.8 fusion.87
  670.0 67.4 %all-gather.25.cloned.1.call-done = bf16[2048,2048]{1,0:T(8,128)(2,1)} async-done(((bf16[2048,256]{1,0:T(8,128)(2,1)}), bf16[2048,2048]{1,0:T(8,128)(2,1)}) %all-gather.25.cloned.1.call-update) | async-done | bytes 8388624 | tf_op jit(solution)/shard_map/all_gather | solution.py:129
  737.4 17.3 fusion.85
  755.4 294.8 %all-gather.29.cloned.1.call-done = f32[4096,2048]{1,0:T(8,128)} async-done(((f32[1024,2048]{1,0:T(8,128)}), f32[4096,2048]{1,0:T(8,128)}) %all-gather.29.cloned.1.call-update) | async-done | bytes 33554448 | tf_op jit(solution)/shard_map/all_gather | solution.py:32
  1050.3 16.3 reduce_sum.327
  1088.2 23.6 %fusion.94 = (bf16[2048]{0:T(1024)(128)(2,1)}, bf16[1024,2048]{1,0:T(8,128)(2,1)}) fusion(bf16[2048,2048]{1,0:T(8,128)(2,1)} %all-gather.25.cloned.1.call-done, f32[1024,2048]{1,0:T(8,128)} %get-tuple-element.655, f32[1024]{0:T(1024)S(1)} %negate_multiply_fusion.1, f32[1024,2048]{1,0:T(8,128)} %fusion.87, f32[2048]{0:T(1024)S(1)} %copy-done.57), kind=kOutput, calls=%fused_computation.149 | convolution fusion | flops 8648652800 | bytes 29376512 | tf_op jit(solution)/shard_map/td,fd->tf/dot_general | solution.py:145
  1111.8 14.5 fusion.95
  1126.4 20.8 convolution_convert_fusion
  1147.3 16.6 convolution_convert_fusion.1
  1163.9 259.8 %all-gather.31.cloned.1.call-done = f32[4096,2048]{1,0:T(8,128)} async-done(((f32[1024,2048]{1,0:T(8,128)}), f32[4096,2048]{1,0:T(8,128)}) %all-gather.31.cloned.1.call-update) | async-done | bytes 33554448 | tf_op jit(solution)/shard_map/all_gather | solution.py:32
  1423.7 16.8 reduce_sum.332
  1475.0 217.7 %while.32 = (s32[]{:T(128)}, f32[2048,4,128]{0,2,1:T(8,128)}, f32[2048,4,128]{0,2,1:T(8,128)}, bf16[2,512,4,128]{3,1,2,0:T(8,128)(2,1)}, bf16[2,512,4,128]{3,1,2...) while((s32[]{:T(128)}, f32[2048,4,128]{0,2,1:T(8,128)}, ...), condition=%wide.region_19.20_spmd.clone.clone.clone, body=%wide.region_17.19_spmd.clone.clone.clone.sunk | while | flops 5443420160 | bytes 264313680 | solution.py:204
  1511.6 14.4 select_select_fusion.7
  1546.6 12.3 multiply_convert_fusion.5
  1619.3 14.4 select_select_fusion.7
  1654.2 12.0 multiply_convert_fusion.5
  1680.9 11.7 bitcast_add_fusion.5
  1715.1 47.0 %select_reduce_fusion.4 = (bf16[1024,512]{0,1:T(8,128)(2,1)}, bf16[1024,512]{0,1:T(8,128)(2,1)}, f32[1024,512]{0,1:T(8,128)S(1)}, f32[1024,512]{0,1:T(8,128)S(1)...) fusion(f32[2,1024,512]{1,0,2:T(2,128)} %reshape.188, pred[2]{0:T(512)(128)(4,1)S(1)} %copy-done.51, ...), kind=kLoop, calls=%fused_computation.97 | loop fusion | flops 9437184 | bytes 16777222 | tf_op jit(solution)/shard_map/reduce_sum | solution.py:213
  1774.1 14.0 collective-permute-start.4
  1827.2 38.7 %reduce-scatter.9.cloned.1.call-done = bf16[256,512]{0,1:T(8,128)(2,1)} async-done(((bf16[2048,512]{0,1:T(8,128)(2,1)}), bf16[256,512]{0,1:T(8,128)(2,1)}) %reduce-scatter.9.cloned.1.call-update) | async-done | bytes 262160 | tf_op jit(solution)/shard_map/reduce_scatter | solution.py:241
  1867.8 295.8 %all-gather.33.cloned.1.call-done = f32[4096,2048]{1,0:T(8,128)} async-done(((f32[1024,2048]{1,0:T(8,128)}), f32[4096,2048]{1,0:T(8,128)}) %all-gather.33.cloned.1.call-update) | async-done | bytes 33554448 | tf_op jit(solution)/shard_map/all_gather | solution.py:32
  2163.6 16.0 reduce_sum.341
  2189.7 28.6 %all-reduce = (bf16[512]{0:T(512)(128)(2,1)S(1)}, bf16[512]{0:T(512)(128)(2,1)S(1)}, bf16[2048]{0:T(1024)(128)(2,1)S(1)}, bf16[2048]{0:T(1024)(128)(2,1)S(1)}, b...) all-reduce(bf16[512]{0:T(512)(128)(2,1)S(1)} %bitcast.125, ...), channel_id=1, replica_groups=mesh['dp'=8,'tensor'=4] {'dp'}, use_global_device_ids=true, to_apply=%region_31.32 | all-reduce | flops 15360 | bytes 61440 | tf_op jit(solution)/shard_map/psum | solution.py:262
  (346 shorter events, 467.4 us)
Async XLA Ops:
  7.2 34.8 %all-gather.17.cloned.1.call-start = ((), (), s32[]{:S(2)}) async-start(), calls=%async_computation.7 | async-start | bytes 2359296 | tf_op jit(solution)/shard_map/all_gather | solution.py:80
  9.0 68.8 %all-gather.19.cloned.1.call-start = ((), (), s32[]{:S(2)}) async-start(), calls=%async_computation.8 | async-start | bytes 2359296 | tf_op jit(solution)/shard_map/all_gather | solution.py:81
  10.9 106.2 %all-gather.15.cloned.1.call-start = ((), (), s32[]{:S(2)}) async-start(), calls=%async_computation.6 | async-start | bytes 2359296 | tf_op jit(solution)/shard_map/all_gather | solution.py:79
  12.7 249.3 %all-gather.21.cloned.1.call-start = ((), (), s32[]{:S(2)}) async-start(), calls=%async_computation.9 | async-start | bytes 2359296 | tf_op jit(solution)/shard_map/all_gather | solution.py:82
  14.6 555.4 %all-gather.27.cloned.1.call-start = ((), (), s32[]{:S(2)}) async-start(), calls=%async_computation.18 | async-start | bytes 41943040 | tf_op jit(solution)/shard_map/all_gather | solution.py:32
  14.6 63.2 %copy-start.58 = (f32[512]{0:T(512)S(1)}, f32[512]{0:T(512)}, u32[]{:S(2)}) copy-start(f32[512]{0:T(512)} %param.31) | copy-start | bytes 6148
  47.3 69.9 %copy-start.59 = (f32[512]{0:T(512)S(1)}, f32[512]{0:T(512)}, u32[]{:S(2)}) copy-start(f32[512]{0:T(512)} %param.30) | copy-start | bytes 6148
  47.3 80.9 %collective-permute-start = (bf16[1024,512]{1,0:T(8,128)(2,1)S(1)}, bf16[1024,512]{1,0:T(8,128)(2,1)S(1)}, u32[]{:S(2)}, u32[]{:S(2)}) collective-permute-start(bf16[1024,512]{1,0:T(8,128)(2,1)S(1)} %convolution_convert_fusion.7), channel_id=1, source_target_pairs={{0,4},{4,8},{8,12},{12,16},{16,20},{20,24},{24,28},{1,5},{5,9},{9,... | collective-permute-start | bytes 3145736 | tf_op jit(solution)/shard_map/ppermute | solution.py:14
  49.6 78.6 %collective-permute-start.1 = (bf16[1024,512]{1,0:T(8,128)(2,1)S(1)}, bf16[1024,512]{1,0:T(8,128)(2,1)}, u32[]{:S(2)}, u32[]{:S(2)}) collective-permute-start(bf16[1024,512]{1,0:T(8,128)(2,1)S(1)} %convolution_convert_fusion.7), channel_id=1, source_target_pairs={{4,0},{8,4},{12,8},{16,12},{20,16},{24,20},{28,24},{5,1},{9,5},{13... | collective-permute-start | bytes 3145736 | tf_op jit(solution)/shard_map/ppermute | solution.py:14
  83.1 45.2 %collective-permute-start.2 = (bf16[1024,512]{1,0:T(8,128)(2,1)S(1)}, bf16[1024,512]{1,0:T(8,128)(2,1)}, u32[]{:S(2)}, u32[]{:S(2)}) collective-permute-start(bf16[1024,512]{1,0:T(8,128)(2,1)S(1)} %add_convert_fusion.4), channel_id=1, source_target_pairs={{0,4},{4,8},{8,12},{12,16},{16,20},{20,24},{24,28},{1,5},{5,9},{9,... | collective-permute-start | bytes 3145736 | tf_op jit(solution)/shard_map/ppermute | solution.py:14
  86.2 42.0 %collective-permute-start.3 = (bf16[1024,512]{1,0:T(8,128)(2,1)S(1)}, bf16[1024,512]{1,0:T(8,128)(2,1)}, u32[]{:S(2)}, u32[]{:S(2)}) collective-permute-start(bf16[1024,512]{1,0:T(8,128)(2,1)S(1)} %add_convert_fusion.4), channel_id=1, source_target_pairs={{4,0},{8,4},{12,8},{16,12},{20,16},{24,20},{28,24},{5,1},{9,5},{13... | collective-permute-start | bytes 3145736 | tf_op jit(solution)/shard_map/ppermute | solution.py:14
  258.2 329.1 %copy-start.6 = (bf16[1024,512]{1,0:T(8,128)(2,1)}, bf16[1024,512]{1,0:T(8,128)(2,1)S(1)}, u32[]{:S(2)}) copy-start(bf16[1024,512]{1,0:T(8,128)(2,1)S(1)} %get-tuple-element.1002) | copy-start | bytes 3145732
  258.3 329.1 %copy-start.11 = (bf16[1024,512]{1,0:T(8,128)(2,1)}, bf16[1024,512]{1,0:T(8,128)(2,1)S(1)}, u32[]{:S(2)}) copy-start(bf16[1024,512]{1,0:T(8,128)(2,1)S(1)} %get-tuple-element.1027) | copy-start | bytes 3145732
  269.8 384.4 %all-gather.23.cloned.1.call-start = ((), (), s32[]{:S(2)}) async-start(), calls=%async_computation.10 | async-start | bytes 9437184 | tf_op jit(solution)/shard_map/all_gather | solution.py:128
  272.6 464.8 %all-gather.25.cloned.1.call-start = ((), (), s32[]{:S(2)}) async-start(), calls=%async_computation.11 | async-start | bytes 9437184 | tf_op jit(solution)/shard_map/all_gather | solution.py:129
  275.3 774.9 %all-gather.29.cloned.1.call-start = ((), (), s32[]{:S(2)}) async-start(), calls=%async_computation.19 | async-start | bytes 41943040 | tf_op jit(solution)/shard_map/all_gather | solution.py:32
  593.1 61.0 %copy-start.33 = (f32[2048]{0:T(1024)S(1)}, f32[2048]{0:T(1024)}, u32[]{:S(2)}) copy-start(f32[2048]{0:T(1024)} %param.34) | copy-start | bytes 24580
  593.1 61.0 %copy-start.47 = (f32[2048]{0:T(1024)S(1)}, f32[2048]{0:T(1024)}, u32[]{:S(2)}) copy-start(f32[2048]{0:T(1024)} %param.35) | copy-start | bytes 24580
  598.1 139.3 %copy-start.57 = (f32[2048]{0:T(1024)S(1)}, f32[2048]{0:T(1024)}, u32[]{:S(2)}) copy-start(f32[2048]{0:T(1024)} %param.37) | copy-start | bytes 24580
  754.7 669.0 %all-gather.31.cloned.1.call-start = ((), (), s32[]{:S(2)}) async-start(), calls=%async_computation.20 | async-start | bytes 41943040 | tf_op jit(solution)/shard_map/all_gather | solution.py:32
  1126.3 686.5 %reduce-scatter.17.cloned.1.call-start = ((), (), s32[]{:S(2)}) async-start(), calls=%async_computation.17 | async-start | bytes 9437184 | tf_op jit(solution)/shard_map/reduce_scatter | solution.py:156
  1147.2 668.4 %reduce-scatter.15.cloned.1.call-start = ((), (), s32[]{:S(2)}) async-start(), calls=%async_computation.16 | async-start | bytes 9437184 | tf_op jit(solution)/shard_map/reduce_scatter | solution.py:153
  1163.8 655.9 %reduce-scatter.13.cloned.1.call-start = ((), (), s32[]{:S(2)}) async-start(), calls=%async_computation.15 | async-start | bytes 2359296 | tf_op jit(solution)/shard_map/reduce_scatter | solution.py:247
  1473.8 347.8 %reduce-scatter.7.cloned.1.call-start = ((), (), s32[]{:S(2)}) async-start(), calls=%async_computation.12 | async-start | bytes 2359296 | tf_op jit(solution)/shard_map/reduce_scatter | solution.py:238
  1701.7 123.7 %reduce-scatter.11.cloned.1.call-start = ((), (), s32[]{:S(2)}) async-start(), calls=%async_computation.14 | async-start | bytes 2359296 | tf_op jit(solution)/shard_map/reduce_scatter | solution.py:244
  1715.0 55.2 %copy-start.18 = (bf16[1024,2048]{1,0:T(8,128)(2,1)S(1)}, bf16[1024,2048]{1,0:T(8,128)(2,1)}, u32[]{:S(2)}) copy-start(bf16[1024,2048]{1,0:T(8,128)(2,1)} %param.23) | copy-start | bytes 12582916
  1762.1 4.0 collective-permute-start.6
  1763.8 6.0 collective-permute-start.7
  1774.0 91.9 %reduce-scatter.9.cloned.1.call-start = ((), (), s32[]{:S(2)}) async-start(), calls=%async_computation.13 | async-start | bytes 2359296 | tf_op jit(solution)/shard_map/reduce_scatter | solution.py:241
  1774.1 16.5 collective-permute-start.4
  1788.1 4.8 collective-permute-start.5
  1800.4 363.2 %all-gather.33.cloned.1.call-start = ((), (), s32[]{:S(2)}) async-start(), calls=%async_computation.21 | async-start | bytes 41943040 | tf_op jit(solution)/shard_map/all_gather | solution.py:32
  (64 other events, 572.6 us)
Sparse Core Ops, SparseCore 0:
  10.2 31.7 all-gather.16
  44.2 33.6 all-gather.18
  80.0 37.0 all-gather.14
  119.1 33.7 all-gather.20
  269.9 300.1 all-gather.26
  572.1 82.0 all-gather.22
  656.3 81.0 all-gather.24
  754.8 295.3 all-gather.28
  1126.4 297.1 all-gather.30
  1425.8 89.5 reduce-scatter.16
  1517.8 87.9 reduce-scatter.14
  1607.9 34.1 reduce-scatter.12
  1701.8 35.6 reduce-scatter.6
  1774.1 51.1 reduce-scatter.10
  1827.5 38.4 reduce-scatter.8
  1867.6 295.9 all-gather.32
